TPU v7x, 32 devices: a whole 2x2x4 slice. The times are simulated.
32 devices in a mesh: seq: 8 (over z, y), head: 4 (over x, core).
Axes of the slice: x: 2, y: 2, z: 4, core: 2. Of those that a mesh axis runs over, the one named last changes fastest.
Arguments:
- prompt_tokens: bfloat16 [2, 2048, 8192], P(None, ('seq', 'head')), may hold values from -6 to 6
- prompt_write: bfloat16 [2, 2048, 1024], P(None, 'seq', 'head'), may hold values from -0.47851562 to 0.47851562
- prompt_read: bfloat16 [2, 2048, 1024], P(None, 'seq', 'head'), may hold values from -0.47851562 to 0.47851562
- prompt_decay: float32 [2, 128, 2048], P(None, 'head', 'seq'), may hold values from -1 to 0, as said below
- prompt_cotangent: bfloat16 [2, 2048, 8192], P(None, 'seq', 'head'), may hold values from -6 to 6
- answer_tokens: bfloat16 [8, 256, 8192], P('seq', 'head'), may hold values from -6 to 6
- answer_write: bfloat16 [8, 256, 1024], P('seq', None, 'head'), may hold values from -0.47851562 to 0.47851562
- answer_read: bfloat16 [8, 256, 1024], P('seq', None, 'head'), may hold values from -0.47851562 to 0.47851562
- answer_decay: float32 [8, 128, 256], P('seq', 'head'), may hold values from -1 to 0, as said below
- answer_cotangent: bfloat16 [8, 256, 8192], P('seq', None, 'head'), may hold values from -6 to 6
- group_sizes: int32 [2], replicated, may hold values from 2 to 6, as said below
- answer_lengths: int32 [8], P('seq'), may hold values from 1 to 256, 1280 in all
Outputs:
- prompt_output: bfloat16 [2, 2048, 8192], P(None, 'seq', 'head')
- prompt_tokens_adjoint: bfloat16 [2, 2048, 8192], P(None, ('seq', 'head'))
- prompt_write_adjoint: bfloat16 [2, 2048, 1024], P(None, 'seq', 'head')
- prompt_read_adjoint: bfloat16 [2, 2048, 1024], P(None, 'seq', 'head')
- prompt_decay_adjoint: float32 [2, 128, 2048], P(None, 'head', 'seq')
- answer_output: bfloat16 [8, 256, 8192], P('seq', None, 'head')
- answer_tokens_adjoint: bfloat16 [8, 256, 8192], P('seq', 'head')
- answer_write_adjoint: bfloat16 [8, 256, 1024], P('seq', None, 'head')
- answer_read_adjoint: bfloat16 [8, 256, 1024], P('seq', None, 'head')
- answer_decay_adjoint: float32 [8, 128, 256], P('seq', 'head')
Inputs may be any that keep to these rules, and one draw needn't show every extreme that they name: Completions are stored in prompt order: the first group_sizes[0] completions follow prompt 0, the next group_sizes[1] prompt 1, and so on; the sizes sum to 8, and one prompt has exactly 6. Completion i has loss and outputs at its first answer_lengths[i] positions only. `prompt_decay`: log decays are negative. `answer_decay`: log decays are negative.
All inputs are finite; a program needn't handle non-finite values. No bound on the sum of `answer_lengths` on one device may be relied on, other than what follows from the above.
Results may differ from a plain program's by a relative error of at most 0.015.
Values may be sent and summed in bfloat16 or wider, within the bound.
A program may use at most 128 MiB of HBM per device.

v0:
```python
from functools import partial

import jax
import jax.numpy as jnp
from jax import lax
from jax.sharding import PartitionSpec as P

HEAD_DIM = 64
STATE = 128
BLOCK = 256


def spread_2(value, axis, source):
    kept = jnp.where(lax.axis_index(axis) == source, value, 0).astype(value.dtype)
    return lax.psum(kept, axis)


def contract(pattern, first_operand, second_operand):
    return jnp.einsum(pattern, first_operand, second_operand, preferred_element_type=jnp.float32)


def block_running(log_decay, groups, block_size):
    head_count, total_length = log_decay.shape
    per_group = head_count // groups
    blocks = total_length // block_size
    return jnp.cumsum(
        log_decay.reshape(groups, per_group, blocks, block_size).transpose(2, 0, 1, 3), axis=3
    )


def ssd_scan(tokens, key_inputs, query_inputs, log_decay, initial, block_size):
    total_length = tokens.shape[0]
    head_count, state_size, head_size = initial.shape
    groups = key_inputs.shape[1] // state_size
    per_group = head_count // groups
    blocks = total_length // block_size
    values = tokens.reshape(blocks, block_size, groups, per_group, head_size)
    key_rows = key_inputs.reshape(blocks, block_size, groups, state_size)
    queries = query_inputs.reshape(blocks, block_size, groups, state_size)
    running = block_running(log_decay, groups, block_size)
    closing = running[..., -1]
    scores = contract("cign,cjgn->cgij", queries, key_rows)
    causal = lax.broadcasted_iota(jnp.int32, (block_size, block_size), 0) >= lax.broadcasted_iota(
        jnp.int32, (block_size, block_size), 1
    )
    spread = running[..., :, None] - running[..., None, :]
    weights = jnp.where(causal, jnp.exp(jnp.where(causal, spread, 0.0)), 0.0)
    mixing = (weights * scores[:, :, None]).astype(jnp.bfloat16)
    inside = contract("cghij,cjghp->cighp", mixing, values)
    to_close = jnp.exp(closing[..., None] - running).transpose(0, 3, 1, 2)
    weighted = (values.astype(jnp.float32) * to_close[..., None]).astype(jnp.bfloat16)
    block_states = contract("cjgn,cjghp->cghnp", key_rows, weighted)

    def ssd_advance(carried, scan_item):
        fresh_state, factor = scan_item
        return (jnp.exp(factor)[..., None, None] * carried + fresh_state, carried)

    ending, starting = lax.scan(
        ssd_advance,
        initial.reshape(groups, per_group, state_size, head_size),
        (block_states, closing),
    )
    outside = contract("cign,cghnp->cighp", queries, starting.astype(jnp.bfloat16))
    outside = outside * jnp.exp(running).transpose(0, 3, 1, 2)[..., None]
    output = (inside + outside).reshape(total_length, head_count * head_size)
    return (output, ending.reshape(head_count, state_size, head_size))


def chain_end(tokens, key_inputs, log_decay, block_size):
    total_length = tokens.shape[0]
    head_count = log_decay.shape[0]
    groups = key_inputs.shape[1] // STATE
    per_group = head_count // groups
    blocks = total_length // block_size
    values = tokens.reshape(blocks, block_size, groups, per_group, HEAD_DIM)
    key_rows = key_inputs.reshape(blocks, block_size, groups, STATE)
    running = block_running(log_decay, groups, block_size)
    closing = running[..., -1]
    to_close = jnp.exp(closing[..., None] - running).transpose(0, 3, 1, 2)
    weighted = (values.astype(jnp.float32) * to_close[..., None]).astype(jnp.bfloat16)
    block_states = contract("cjgn,cjghp->cghnp", key_rows, weighted)

    def chain_advance(carried, scan_item):
        fresh_state, factor = scan_item
        return (jnp.exp(factor)[..., None, None] * carried + fresh_state, None)

    blank = jnp.zeros((groups, per_group, STATE, HEAD_DIM), jnp.float32)
    ending = lax.scan(chain_advance, blank, (block_states, closing))[0]
    return ending.reshape(head_count, STATE, HEAD_DIM)


def start_gradient(query_inputs, log_decay, seed, block_size):
    total_length = seed.shape[0]
    head_count = log_decay.shape[0]
    groups = query_inputs.shape[1] // STATE
    per_group = head_count // groups
    blocks = total_length // block_size
    queries = query_inputs.reshape(blocks, block_size, groups, STATE).astype(jnp.float32)
    running = block_running(log_decay, groups, block_size)
    closing = running[..., -1]
    pulled = (
        seed.reshape(blocks, block_size, groups, per_group, HEAD_DIM)
        * jnp.exp(running).transpose(0, 3, 1, 2)[..., None]
    )
    reaching = jnp.einsum("cign,cighp->cghnp", queries, pulled, precision=lax.Precision.HIGHEST)
    reaching = reaching.astype(jnp.bfloat16).astype(jnp.float32)

    def retreat(carried, scan_item):
        fresh_grad, factor = scan_item
        return (fresh_grad + jnp.exp(factor)[..., None, None] * carried, None)

    blank = jnp.zeros((groups, per_group, STATE, HEAD_DIM), jnp.float32)
    total = lax.scan(retreat, blank, (reaching, closing), reverse=True)[0]
    return total.reshape(head_count, STATE, HEAD_DIM)


def per_device(
    prompt_tokens,
    prompt_write,
    prompt_read,
    prompt_decay,
    prompt_cotangent,
    answer_tokens,
    answer_write,
    answer_read,
    answer_decay,
    answer_cotangent,
    group_sizes,
    answer_lengths,
):
    prompt_local, answer_local = (
        lax.all_to_all(prompt_tokens, "head", split_axis=2, concat_axis=1, tiled=True),
        lax.all_to_all(answer_tokens, "head", split_axis=2, concat_axis=1, tiled=True),
    )
    prompts = prompt_decay.shape[0]
    local_heads = prompt_decay.shape[1]
    answers_here = answer_decay.shape[0]
    batched = jax.vmap(partial(ssd_scan, block_size=BLOCK))
    position = lax.axis_index("seq")
    devices = lax.axis_size("seq")
    blank = jnp.zeros((prompts, local_heads, STATE, HEAD_DIM), jnp.float32)
    closing_decay = jnp.exp(jnp.sum(prompt_decay, axis=2))
    local_end = jax.vmap(partial(chain_end, block_size=BLOCK))(
        prompt_local, prompt_write, prompt_decay
    )
    every_decay, every_end = (
        lax.all_gather(closing_decay[None], "seq", axis=0, tiled=True),
        lax.all_gather(local_end[None], "seq", axis=0, tiled=True),
    )

    def absorb_forward(counter, carried):
        applied = every_decay[counter][..., None, None] * carried + every_end[counter]
        return jnp.where(counter < position, applied, carried)

    incoming = lax.fori_loop(0, devices, absorb_forward, blank)
    (prompt_result, prompt_end), prompt_pull = jax.vjp(
        batched, prompt_local, prompt_write, prompt_read, prompt_decay, incoming
    )
    final_state = spread_2(prompt_end.astype(jnp.bfloat16), "seq", devices - 1).astype(
        prompt_end.dtype
    )
    slots = position * answers_here + jnp.arange(answers_here, dtype=jnp.int32)
    bounds = jnp.cumsum(group_sizes)
    owner = jnp.sum((slots[:, None] >= bounds[None, :]).astype(jnp.int32), axis=1)
    selector = (owner[:, None] == jnp.arange(prompts, dtype=jnp.int32)[None, :]).astype(jnp.float32)
    answer_start = jnp.einsum(
        "aq,qhnp->ahnp", selector, final_state, precision=lax.Precision.HIGHEST
    )
    live = jnp.arange(answer_local.shape[1], dtype=jnp.int32)[None, :] < answer_lengths[:, None]
    (answer_result, answer_end), answer_pull = jax.vjp(
        batched, answer_local, answer_write, answer_read, answer_decay, answer_start
    )
    answer_seed = jnp.where(
        live[..., None], answer_cotangent, jnp.zeros_like(answer_cotangent)
    ).astype(jnp.float32)
    answer_grads = answer_pull((answer_seed, jnp.zeros_like(answer_end)))
    start_local = jnp.einsum(
        "aq,ahnp->qhnp", selector, answer_grads[4], precision=lax.Precision.HIGHEST
    )
    final_grad = lax.psum(start_local.astype(jnp.bfloat16), "seq").astype(jnp.float32)
    prompt_seed = prompt_cotangent.astype(jnp.float32)
    start_grad = jax.vmap(partial(start_gradient, block_size=BLOCK))(
        prompt_read, prompt_decay, prompt_seed
    )
    every_grad = lax.all_gather(
        start_grad[None].astype(jnp.bfloat16), "seq", axis=0, tiled=True
    ).astype(jnp.float32)

    def absorb_backward(counter, carried):
        source = devices - 1 - counter
        applied = every_decay[source][..., None, None] * carried + every_grad[source]
        return jnp.where(source > position, applied, carried)

    end_grad = lax.fori_loop(0, devices, absorb_backward, final_grad)
    prompt_grads = prompt_pull((prompt_seed, end_grad))
    token_back = (
        lax.all_to_all(prompt_grads[0], "head", split_axis=1, concat_axis=2, tiled=True),
        lax.all_to_all(answer_grads[0], "head", split_axis=1, concat_axis=2, tiled=True),
    )
    answer_output = jnp.where(live[..., None], answer_result, 0.0).astype(jnp.bfloat16)
    return (
        prompt_result.astype(jnp.bfloat16),
        token_back[0],
        prompt_grads[1],
        prompt_grads[2],
        prompt_grads[3],
        answer_output,
        token_back[1],
        answer_grads[1],
        answer_grads[2],
        answer_grads[3],
    )


def solution(mesh):
    return jax.shard_map(
        per_device,
        mesh=mesh,
        in_specs=(
            P(None, ("seq", "head"), None),
            P(None, "seq", "head"),
            P(None, "seq", "head"),
            P(None, "head", "seq"),
            P(None, "seq", "head"),
            P("seq", "head", None),
            P("seq", None, "head"),
            P("seq", None, "head"),
            P("seq", "head", None),
            P("seq", None, "head"),
            P(),
            P("seq"),
        ),
        out_specs=(
            P(None, "seq", "head"),
            P(None, ("seq", "head"), None),
            P(None, "seq", "head"),
            P(None, "seq", "head"),
            P(None, "head", "seq"),
            P("seq", None, "head"),
            P("seq", "head", None),
            P("seq", None, "head"),
            P("seq", None, "head"),
            P("seq", "head", None),
        ),
        check_vma=False,
    )
```

profile of v0, /device:TPU:0, one launch (start us, length us, event | category | flops | bytes accessed | tf_op | source)
XLA Modules:
  0.0 861.1 jit_solution(100581066148840668)
XLA Ops:
  7.2 9.5 %copy.431 = bf16[2,64,8192]{1,0,2:T(2,128)(2,1)} copy(bf16[2,64,8192]{2,1,0:T(8,128)(2,1)} %param.16) | data formatting | bytes 4194304 | tf_op args[0]
  44.2 9.2 %all-to-all-done = bf16[4,2,131072]{2,1,0:T(2,128)(2,1)} async-done(((bf16[4,2,131072]{2,1,0:T(2,128)(2,1)}), bf16[4,2,131072]{2,1,0:T(2,128)(2,1)}, u32[]{:S(2)}, u32[]{:S(2)}) %all-to-all-start) | async-done | bytes 2097184 | tf_op jit(solution)/shard_map/all_to_all | solution.py:132
  59.3 9.1 %copy.432 = bf16[2,64,4,2048]{3,1,2,0:T(8,128)(2,1)S(1)} copy(bf16[2,64,4,2048]{1,0,3,2:T(2,128)(2,1)} %bitcast.444) | data formatting | bytes 4194304 | tf_op jit(solution)/shard_map/all_to_all | solution.py:132
  91.9 9.2 %copy.480 = bf16[1,64,8192]{1,0,2:T(2,128)(2,1)} copy(bf16[1,64,8192]{2,1,0:T(8,128)(2,1)} %param.21) | data formatting | bytes 2097152 | tf_op args[5]
  101.7 46.5 %reduce.29 = bf16[8192,64]{1,0:T(8,128)(2,1)} reduce(bf16[8192,1,64]{2,1,0:T(2,128)(2,1)} %bitcast.442, bf16[]{:T(256)} %broadcast.302), dimensions={1}, to_apply=%bitcast.391.reduce_sub_computation | reduce | bytes 2097154
  190.7 22.6 %all-gather.1 = f32[8,2,32]{2,1,0:T(2,128)S(1)} all-gather(f32[1,2,32]{2,1,0:T(2,128)S(1)} %exponential_bitcast_fusion.2), channel_id=2, replica_groups=mesh['seq'=8,'head'=4] {'seq'}, dimensions={0}, use_global_device_ids=true | all-gather | bytes 2304 | tf_op jit(solution)/shard_map/all_gather | solution.py:147
  252.8 7.4 fusion.17
  280.6 7.8 reshape.986
  288.4 8.0 copy.467
  296.4 23.5 %all-gather.5.cloned.1.call-done = f32[8,2,32,128,64]{3,4,2,1,0:T(8,128)} async-done(((f32[1,2,32,128,64]{3,4,2,1,0:T(8,128)}), f32[8,2,32,128,64]{3,4,2,1,0:T(8,128)}) %all-gather.5.cloned.1.call-update) | async-done | bytes 16777232 | tf_op jit(solution)/shard_map/all_gather | solution.py:148
  319.9 83.3 %while.20 = (s32[]{:T(128)}, f32[2,32,128,64]{3,2,1,0:T(8,128)}, s32[]{:T(128)}, f32[8,2,32]{2,1,0:T(2,128)S(1)}, f32[8,2,32,128,64]{3,4,2,1,0:T(8,128)}, /*index=5*/s32[]{:T(128)}, s32[]{:T(128)}) while((s32[]{:T(128)}, f32[2,32,128,64]{3,2,1,0:T(8,128)}, s32[]{:T(128)}, f32[8,2,32]{2,1,0:T(2,128)S(1)}, ...), condition=%wide.region_4.5_spmd.clone, body=%wide.region_3.4_spmd.clone.sunk | while | flops 2097156 | bytes 14680945 | solution.py:155
  333.7 6.0 fusion.191
  344.2 6.0 fusion.191
  354.6 6.0 fusion.191
  365.1 6.0 fusion.191
  376.2 6.0 fusion.191
  386.6 6.0 fusion.191
  397.1 6.0 fusion.191
  410.3 12.4 %fusion.8 = (f32[2,2,16,256]{3,2,1,0:T(8,128)}, f32[2,2,16,256]{3,2,1,0:T(8,128)S(1)}, bf16[2,2,256,256]{3,2,1,0:T(8,128)(2,1)S(1)}) fusion(f32[2,2,256,256]{3,2,1,0:T(8,128)} %fusion.158, f32[2,2,16,256]{3,2,1,0:T(8,128)S(1)} %copy-done.49, pred[256,256]{1,0:T(8,128)(4,1)} %iota_compare_fusion, bf16[2,2,16,64,256]{4,3,2,1,0:T(8,128)(2,1)S(1)} %bitcast.452, ...), kind=kOutput, calls=%fused_computation.18 | convolution fusion | flops 591101952 | bytes 6029312 | tf_op jit(solution)/shard_map/transpose(jvp(vmap(cghij,cjghp->cighp)))/dot_general | solution.py:19
  427.5 17.7 %all-gather.7.cloned.1.call-done = bf16[8,2,32,128,64]{3,4,2,1,0:T(8,128)(2,1)} async-done(((bf16[1,2,32,128,64]{3,4,2,1,0:T(8,128)(2,1)}), bf16[8,2,32,128,64]{3,4,2,1,0:T(8,128)(2,1)}) %all-gather.7.cloned.1.call-update) | async-done | bytes 8388624 | tf_op jit(solution)/shard_map/all_gather | solution.py:185
  445.3 12.1 %convert_element_type.317 = f32[8,2,32,128,64]{3,4,2,1,0:T(8,128)} convert(bf16[8,2,32,128,64]{3,4,2,1,0:T(8,128)(2,1)} %all-gather.7.cloned.1.call-done) | non-fusion elementwise | flops 4194304 | bytes 25165824 | tf_op jit(solution)/shard_map/convert_element_type | solution.py:187
  457.4 146.9 %all-reduce.5.cloned.1.call-done = (bf16[2,32,128,64]{3,2,1,0:T(8,128)(2,1)}, bf16[2,32,128,64]{3,2,1,0:T(8,128)(2,1)}) async-done(((bf16[2,32,128,64]{3,2,1,0:T(8,128)(2,1)}, bf16[2,32,128,64]{3,2,1,0:T(8,128)(2,1)}), (bf16[2,32,128,64]{3,2,1,0:T(8,128)(2,1)}, bf16[2,32,128,64]{3,2,1,0:T(8,128)(2,1)})) %all-reduce.5.cloned.1.call-update) | async-done | bytes 2097168 | tf_op jit(solution)/shard_map/psum | solution.py:180
  608.3 83.2 %while.19 = (s32[]{:T(128)}, f32[2,32,128,64]{3,2,1,0:T(8,128)}, s32[]{:T(128)}, f32[8,2,32]{2,1,0:T(2,128)S(1)}, f32[8,2,32,128,64]{3,4,2,1,0:T(8,128)}, /*index=5*/s32[]{:T(128)}, s32[]{:T(128)}, s32[]{:T(128)}, s32[]{:T(128)}) while((s32[]{:T(128)}, f32[2,32,128,64]{3,2,1,0:T(8,128)}, s32[]{:T(128)}, f32[8,2,32]{2,1,0:T(2,128)S(1)}, ...), condition=%wide.region_11.12_spmd, body=%wide.region_10.11_spmd.sunk | while | flops 1572871 | bytes 14680997 | solution.py:194
  644.0 5.9 fusion.190
  716.4 9.9 %reduce-window.35 = f32[2,1,2,16,2,128]{5,3,4,2,1,0:T(8,128)S(1)} reduce-window(f32[2,1,2,16,2,128]{5,3,4,2,1,0:T(8,128)S(1)} %copy.473, f32[]{:T(128)} %constant.173.clone.1), window={size=1x1x1x1x1x128 pad=0_0x0_0x0_0x0_0x0_0x0_127}, to_apply=%region_19.20 | reduce-window | flops 2080768 | bytes 131076 | tf_op jit(solution)/shard_map/reduce-window.5
  735.5 7.2 fusion.20
  746.8 8.8 %fusion.38 = bf16[2,1,256,2,16,64]{2,5,4,3,0,1:T(8,128)(2,1)} fusion(bf16[2,2,16,64,256]{4,3,2,1,0:T(8,128)(2,1)} %get-tuple-element.523, f32[2,256,2,16]{1,3,2,0:T(8,128)S(1)} %copy-done.48, bf16[2,2,16,64,256]{4,3,2,1,0:T(8,128)(2,1)S(1)} %bitcast.453, f32[2,2,256,256]{3,2,1,0:T(8,128)} %fusion.158, f32[2,2,16,256]{3,2,1,0:T(8,128)S(1)} %copy-done.50, ...), kind=kOutput, calls=%fused_computation.63 | convolution fusion | flops 563085312 | bytes 7536640 | tf_op jit(solution)/shard_map/transpose(jvp(vmap(cghij,cjghp->cighp)))/dot_general | solution.py:19
  755.6 6.3 copy.458
  782.5 6.0 copy.489
  788.5 9.1 %reduce.30 = bf16[256,2048]{1,0:T(8,128)(2,1)} reduce(bf16[256,1,2048]{2,1,0:T(2,128)(2,1)} %bitcast.457, bf16[]{:T(256)} %broadcast.302), dimensions={1}, to_apply=%bitcast.393.reduce_sub_computation | reduce | bytes 2097154
  811.8 8.2 all-to-all-done.3
  843.2 7.2 all-to-all-done.1
  (355 shorter events, 392.6 us)
Async XLA Ops:
  16.7 10.5 %copy-start.45 = (f32[2,32,256]{2,1,0:T(8,128)S(1)}, f32[2,32,256]{2,1,0:T(8,128)}, u32[]{:S(2)}) copy-start(f32[2,32,256]{2,1,0:T(8,128)} %param.19) | copy-start | bytes 196612
  22.6 30.8 %all-to-all-start = ((bf16[4,2,131072]{2,1,0:T(2,128)(2,1)}), bf16[4,2,131072]{2,1,0:T(2,128)(2,1)}, u32[]{:S(2)}, u32[]{:S(2)}) async-start(bf16[4,2,131072]{2,1,0:T(2,128)(2,1)} %reshape.1035), calls=%async_computation | async-start | bytes 4194304 | tf_op jit(solution)/shard_map/all_to_all | solution.py:132
  27.1 292.8 %all-gather.5.cloned.1.call-start = ((), (), s32[]{:S(2)}) async-start(), calls=%async_computation.4 | async-start | bytes 18874368 | tf_op jit(solution)/shard_map/all_gather | solution.py:148
  37.1 22.1 %copy-start.42 = (f32[2,256,2,16]{1,3,2,0:T(8,128)}, f32[2,256,2,16]{1,3,2,0:T(8,128)S(1)}, u32[]{:S(2)}) copy-start(f32[2,256,2,16]{1,3,2,0:T(8,128)S(1)} %copy.441) | copy-start | bytes 196612
  38.2 118.8 %copy-start.16 = (bf16[2,256,2,128]{3,2,1,0:T(2,128)(2,1)}, bf16[2,256,2,128]{3,2,1,0:T(2,128)(2,1)S(1)}, u32[]{:S(2)}) copy-start(bf16[2,256,2,128]{3,2,1,0:T(2,128)(2,1)S(1)} %reshape.936) | copy-start | bytes 786436
  38.2 21.1 %copy-start.54 = (f32[2,2,16]{2,1,0:T(2,128)}, f32[2,2,16]{2,1,0:T(2,128)S(1)}, u32[]{:S(2)}) copy-start(f32[2,2,16]{2,1,0:T(2,128)S(1)} %get-tuple-element.515) | copy-start | bytes 772
  91.2 354.1 %all-gather.7.cloned.1.call-start = ((), (), s32[]{:S(2)}) async-start(), calls=%async_computation.5 | async-start | bytes 9437184 | tf_op jit(solution)/shard_map/all_gather | solution.py:185
  148.3 12.0 %copy-start.57 = (f32[1,32,256]{2,1,0:T(8,128)S(1)}, f32[1,32,256]{2,1,0:T(8,128)}, u32[]{:S(2)}) copy-start(f32[1,32,256]{2,1,0:T(8,128)} %param.24) | copy-start | bytes 98308
  152.6 71.8 %all-to-all-start.2 = ((bf16[4,2,65536]{2,1,0:T(2,128)(2,1)}), bf16[4,2,65536]{2,1,0:T(2,128)(2,1)}, u32[]{:S(2)}, u32[]{:S(2)}) async-start(bf16[4,2,65536]{2,1,0:T(2,128)(2,1)} %reshape.1037), calls=%async_computation.2 | async-start | bytes 2097152 | tf_op jit(solution)/shard_map/all_to_all | solution.py:133
  156.9 447.4 %all-reduce.5.cloned.1.call-start = ((), (), s32[]{:S(2)}) async-start(), calls=%async_computation.6 | async-start | bytes 8388608 | tf_op jit(solution)/shard_map/psum | solution.py:180
  162.7 11.2 %copy-start.61 = (pred[256]{0:T(512)(128)(4,1)}, pred[256]{0:T(512)(128)(4,1)S(1)}, u32[]{:S(2)}) copy-start(pred[256]{0:T(512)(128)(4,1)S(1)} %iota_compare_fusion.1) | copy-start | bytes 772
  166.6 17.5 %copy-start.4 = (bf16[1,256,2048]{1,2,0:T(8,128)(2,1)}, bf16[1,256,2048]{1,2,0:T(8,128)(2,1)S(1)}, u32[]{:S(2)}) copy-start(bf16[1,256,2048]{1,2,0:T(8,128)(2,1)S(1)} %copy.442) | copy-start | bytes 3145732
  166.6 13.4 %copy-start.63 = (s32[2]{0:T(128)S(1)}, s32[2]{0:T(128)}, u32[]{:S(2)}) copy-start(s32[2]{0:T(128)} %param.26) | copy-start | bytes 28
  173.2 44.7 %copy-start.29 = (bf16[256,2,128]{2,1,0:T(2,128)(2,1)}, bf16[256,2,128]{2,1,0:T(2,128)(2,1)S(1)}, u32[]{:S(2)}) copy-start(bf16[256,2,128]{2,1,0:T(2,128)(2,1)S(1)} %reshape.952) | copy-start | bytes 393220
  186.7 42.6 %copy-start.32 = (bf16[256,2,128]{0,2,1:T(8,128)(2,1)}, bf16[256,2,128]{0,2,1:T(8,128)(2,1)S(1)}, u32[]{:S(2)}) copy-start(bf16[256,2,128]{0,2,1:T(8,128)(2,1)S(1)} %copy.494) | copy-start | bytes 393220
  218.5 49.0 %copy-start.58 = (f32[2,16]{1,0:T(2,128)}, f32[2,16]{1,0:T(2,128)S(1)}, u32[]{:S(2)}) copy-start(f32[2,16]{1,0:T(2,128)S(1)} %slice_bitcast_fusion.5) | copy-start | bytes 388
  252.8 10.7 %copy-start.31 = (bf16[256,2,128]{2,1,0:T(2,128)(2,1)S(1)}, bf16[256,2,128]{2,1,0:T(2,128)(2,1)}, u32[]{:S(2)}) copy-start(bf16[256,2,128]{2,1,0:T(2,128)(2,1)} %reshape.970) | copy-start | bytes 393220
  266.6 11.4 %copy-start.19 = (f32[256,2,16]{2,1,0:T(2,128)}, f32[256,2,16]{2,1,0:T(2,128)S(1)}, u32[]{:S(2)}) copy-start(f32[256,2,16]{2,1,0:T(2,128)S(1)} %copy.497) | copy-start | bytes 98308
  410.3 15.3 %copy-start.23 = (bf16[2,256,2,128]{1,3,2,0:T(8,128)(2,1)S(1)}, bf16[2,256,2,128]{1,3,2,0:T(8,128)(2,1)}, u32[]{:S(2)}) copy-start(bf16[2,256,2,128]{1,3,2,0:T(8,128)(2,1)} %copy.463) | copy-start | bytes 786436
  410.3 16.3 %copy-start.22 = (bf16[2,256,2,128]{1,3,2,0:T(8,128)(2,1)S(1)}, bf16[2,256,2,128]{1,3,2,0:T(8,128)(2,1)}, u32[]{:S(2)}) copy-start(bf16[2,256,2,128]{1,3,2,0:T(8,128)(2,1)} %copy.465) | copy-start | bytes 786436
  726.5 9.0 %copy-start.24 = (bf16[2,256,2,16,64]{1,4,3,2,0:T(8,128)(2,1)S(1)}, bf16[2,256,2,16,64]{1,4,3,2,0:T(8,128)(2,1)}, u32[]{:S(2)}) copy-start(bf16[2,256,2,16,64]{1,4,3,2,0:T(8,128)(2,1)} %copy.433) | copy-start | bytes 6291460
  726.5 9.0 %copy-start.43 = (f32[2,256,2,16]{1,3,2,0:T(8,128)S(1)}, f32[2,256,2,16]{1,3,2,0:T(8,128)}, u32[]{:S(2)}) copy-start(f32[2,256,2,16]{1,3,2,0:T(8,128)} %copy-done.42) | copy-start | bytes 196612
  726.5 9.0 %copy-start.50 = (f32[2,2,16,256]{3,2,1,0:T(8,128)S(1)}, f32[2,2,16,256]{3,2,1,0:T(8,128)}, u32[]{:S(2)}) copy-start(f32[2,2,16,256]{3,2,1,0:T(8,128)} %reduce_window_sum.124) | copy-start | bytes 196612
  788.5 21.1 %copy-start.1 = (bf16[256,2,16,64]{3,2,1,0:T(8,128)(2,1)S(1)}, bf16[256,2,16,64]{3,2,1,0:T(8,128)(2,1)}, u32[]{:S(2)}) copy-start(bf16[256,2,16,64]{3,2,1,0:T(8,128)(2,1)} %reshape.971) | copy-start | bytes 3145732
  801.3 18.8 %all-to-all-start.3 = ((bf16[4,2,65536]{2,1,0:T(2,128)(2,1)}), bf16[4,2,65536]{2,1,0:T(2,128)(2,1)}, u32[]{:S(2)}, u32[]{:S(2)}) async-start(bf16[4,2,65536]{2,1,0:T(2,128)(2,1)} %reshape.1039), calls=%async_computation.3 | async-start | bytes 2097152 | tf_op jit(solution)/shard_map/all_to_all | solution.py:198
  811.8 17.8 %copy-start.28 = (bf16[32,128,64]{1,2,0:T(8,128)(2,1)S(1)}, bf16[32,128,64]{1,2,0:T(8,128)(2,1)}, u32[]{:S(2)}) copy-start(bf16[32,128,64]{1,2,0:T(8,128)(2,1)} %convert_element_type.341) | copy-start | bytes 1572868
  811.8 17.8 %copy-start.47 = (f32[256,2,16]{0,2,1:T(8,128)S(1)}, f32[256,2,16]{0,2,1:T(8,128)}, u32[]{:S(2)}) copy-start(f32[256,2,16]{0,2,1:T(8,128)} %copy.447) | copy-start | bytes 98308
  811.8 18.2 %copy-start.33 = (bf16[256,2,128]{0,2,1:T(8,128)(2,1)S(1)}, bf16[256,2,128]{0,2,1:T(8,128)(2,1)}, u32[]{:S(2)}) copy-start(bf16[256,2,128]{0,2,1:T(8,128)(2,1)} %copy-done.32) | copy-start | bytes 393220
  811.8 18.2 %copy-start.38 = (bf16[2,256,256]{2,1,0:T(8,128)(2,1)S(1)}, bf16[2,256,256]{2,1,0:T(8,128)(2,1)}, u32[]{:S(2)}) copy-start(bf16[2,256,256]{2,1,0:T(8,128)(2,1)} %get-tuple-element.485) | copy-start | bytes 786436
  820.0 30.4 %all-to-all-start.1 = ((bf16[2,256,2048]{2,0,1:T(2,128)(2,1)}), bf16[2,256,2048]{2,0,1:T(2,128)(2,1)}, u32[]{:S(2)}, u32[]{:S(2)}) async-start(bf16[2,256,2048]{2,0,1:T(2,128)(2,1)} %copy.458), calls=%async_computation.1 | async-start | bytes 4194304 | tf_op jit(solution)/shard_map/all_to_all | solution.py:197
  824.7 13.0 %copy-start.14 = (bf16[1,256,2048]{2,1,0:T(8,128)(2,1)S(1)}, bf16[1,256,2048]{2,1,0:T(8,128)(2,1)}, u32[]{:S(2)}) copy-start(bf16[1,256,2048]{2,1,0:T(8,128)(2,1)} %copy.486) | copy-start | bytes 3145732
  824.7 13.0 %copy-start.62 = (pred[256]{0:T(512)(128)(4,1)S(1)}, pred[256]{0:T(512)(128)(4,1)}, u32[]{:S(2)}) copy-start(pred[256]{0:T(512)(128)(4,1)} %copy-done.61) | copy-start | bytes 772
  (39 other events, 199.1 us)
Sparse Core Ops, SparseCore 0:
  91.3 228.5 all-gather.4
  322.6 122.6 all-gather.6
  449.6 154.6 all-reduce.4
where the time goes:
time: 873 us; the launch traced here: 861 us
  local copies, waits for them, and re-layouts  265 us (30%)
  other arithmetic  238 us (27%)
  waiting for transfers between devices  213 us (24%)
  matrix products  88.4 us (10%)
  blocking collectives  22.6 us (3%)
  starting transfers between devices  18.3 us (2%)
  between operations  15.5 us (2%)
    psum x1, waiting for transfers between devices, per_device(): lax.psum(start_local.astype(jnp.bfloat16), 'seq').astype(jnp.float32)  147 us
    dot_general x22, matrix products, contract(): jnp.einsum(pattern, first_operand, second_operand, preferred_element_type...  79.2 us
    unnamed x149, local copies, waits for them, and re-layouts  69.2 us
    unnamed x3, other arithmetic  55.7 us
    select_n x8, other arithmetic, absorb_backward(): return jnp.where(source > position, applied, carried)  47.5 us
    select_n x8, other arithmetic, absorb_forward(): return jnp.where(counter < position, applied, carried)  46.8 us
    another operation x47, local copies, waits for them, and re-layouts  36.9 us
    dynamic_slice x16, local copies, waits for them, and re-layouts, absorb_forward(): every_end[counter]  36.4 us
  transfers between devices with their start and end apart: 7, of which 6 were waited for; matrix products, arithmetic and copies ran while one was open for 39% of the time, Pallas kernels for 0%

commit v1 on v0

v1 whole, which is shorter than its diff:
```python
import jax
import jax.numpy as jnp
from jax import lax
from jax.experimental import pallas as pl
from jax.experimental.pallas import tpu as pltpu
from jax.sharding import PartitionSpec as P

HEAD_DIM = 64
STATE = 128
BLOCK = 256
F32 = jnp.float32
BF16 = jnp.bfloat16
NN = (((1,), (0,)), ((), ()))
NT = (((1,), (1,)), ((), ()))
TN = (((0,), (0,)), ((), ()))
PARAMS = pltpu.CompilerParams(vmem_limit_bytes=56 * 1024 * 1024)


def mm(a, b, dims):
    return lax.dot_general(a, b, dims, preferred_element_type=F32)


def mm_exact(a, b, dims):
    return lax.dot_general(a, b, dims, precision=lax.Precision.HIGHEST, preferred_element_type=F32)


def two_term(value):
    high = value.astype(BF16)
    return high, (value - high.astype(F32)).astype(BF16)


def triangle(size, lower=True):
    row = lax.broadcasted_iota(jnp.int32, (size, size), 0)
    column = lax.broadcasted_iota(jnp.int32, (size, size), 1)
    return jnp.where(row >= column if lower else row < column, 1.0, 0.0).astype(F32)


def running_columns(decay):
    return mm_exact(triangle(decay.shape[1]), decay, NT)


def spread_heads(columns, heads):
    row = lax.broadcasted_iota(jnp.int32, (heads, heads * HEAD_DIM), 0)
    lane = lax.broadcasted_iota(jnp.int32, (heads, heads * HEAD_DIM), 1)
    pick = jnp.where(lane // HEAD_DIM == row, 1.0, 0.0).astype(BF16)
    high, low = two_term(columns)
    return mm(high, pick, NN) + mm(low, pick, NN)


def head_sums(value, heads):
    width = value.shape[1]
    row = lax.broadcasted_iota(jnp.int32, (heads, width), 0)
    lane = lax.broadcasted_iota(jnp.int32, (heads, width), 1)
    pick = jnp.where(lane // HEAD_DIM == row, 1.0, 0.0).astype(BF16)
    high, low = two_term(value)
    return mm(pick, high, NT) + mm(pick, low, NT)


def masked_rows(dy, limit):
    row = lax.broadcasted_iota(jnp.int32, dy.shape, 0)
    return jnp.where(row < limit, dy.astype(F32), 0.0)


def start_grad_kernel(limits, dy_ref, read_ref, decay_ref, out_ref):
    heads = decay_ref.shape[1]
    dy = masked_rows(dy_ref[0], limits[pl.program_id(0)])
    er = spread_heads(jnp.exp(running_columns(decay_ref[0])), heads)
    edy = (er * dy).astype(BF16)
    state = mm(read_ref[0], edy, TN)
    out_ref[:, 0] = state.reshape(out_ref.shape[0], out_ref.shape[2], -1).astype(BF16)


def local_end_kernel(x_ref, write_ref, decay_ref, out_ref):
    heads = decay_ref.shape[1]
    x = x_ref[:, 0].reshape(-1, x_ref.shape[3])
    r = running_columns(decay_ref[0])
    ec = spread_heads(jnp.exp(r[-1:] - r), heads)
    w = (ec * x.astype(F32)).astype(BF16)
    state = mm(write_ref[0], w, TN)
    out_ref[:, 0] = state.reshape(out_ref.shape[0], out_ref.shape[2], -1).astype(BF16)


def inside_kernel(
    limits, x_ref, dy_ref, write_ref, read_ref, decay_ref, y_ref, dx_ref, dw_ref, dr_ref, sum_ref, ds_ref, dy_scr
):
    heads = decay_ref.shape[1]
    length = decay_ref.shape[2]
    decay = decay_ref[0]
    write, read = write_ref[0], read_ref[0]
    dy_scr[...] = masked_rows(dy_ref[0], limits[pl.program_id(0)]).astype(BF16)
    tri = triangle(length)
    r_col = mm_exact(tri, decay, NT)
    r_row = mm_exact(decay, tri, NT)
    scores = mm(read, write, NT)
    causal = lax.broadcasted_iota(jnp.int32, (length, length), 0) >= lax.broadcasted_iota(
        jnp.int32, (length, length), 1
    )
    lane = lax.broadcasted_iota(jnp.int32, (1, 2 * HEAD_DIM), 1)
    half = (
        jnp.where(lane < HEAD_DIM, 1.0, 0.0).astype(BF16),
        jnp.where(lane < HEAD_DIM, 0.0, 1.0).astype(BF16),
    )
    sums = jnp.zeros((heads, length), F32)
    row_id = lax.broadcasted_iota(jnp.int32, (heads, 2 * HEAD_DIM), 0)
    lane_id = lax.broadcasted_iota(jnp.int32, (heads, 2 * HEAD_DIM), 1)
    for pair in range(heads // 2):
        columns = slice(pair * 2 * HEAD_DIM, (pair + 1) * 2 * HEAD_DIM)
        x = x_ref[:, 0, :, columns].reshape(length, 2 * HEAD_DIM)
        dy = dy_scr[:, columns]
        y = jnp.zeros((length, 2 * HEAD_DIM), F32)
        dx = jnp.zeros((length, 2 * HEAD_DIM), F32)
        for one in range(2):
            head = pair * 2 + one
            x_one, dy_one = x * half[one], dy * half[one]
            gap = r_col[:, head : head + 1] - r_row[head : head + 1, :]
            weights = jnp.exp(jnp.where(causal, gap, -1e30))
            mixing = (weights * scores).astype(BF16)
            y = y + mm(mixing, x_one, NN)
            dx = dx + mm(mixing, dy_one, TN)
            pulled = mm(dy_one, x, NT) * weights
            if head == 0:
                ds_ref[...] = pulled
            else:
                ds_ref[...] += pulled
        y_ref[0, :, columns] = y.astype(BF16)
        dx_ref[:, 0, :, columns] = dx.astype(BF16).reshape(dx_ref.shape[0], dx_ref.shape[2], 2 * HEAD_DIM)
        pick = jnp.where(row_id == 2 * pair + lane_id // HEAD_DIM, 1.0, 0.0).astype(BF16)
        high, low = two_term(dy.astype(F32) * y - x.astype(F32) * dx)
        sums = sums + mm(pick, high, NT) + mm(pick, low, NT)
    sum_ref[0] = sums
    ds = ds_ref[...].astype(BF16)
    dr_ref[0] = mm(ds, write, NN).astype(dr_ref.dtype)
    dw_ref[0] = mm(ds, read, TN).astype(dw_ref.dtype)


def chain_kernel(owner, recv_ref, out_ref, *, prompts, answers):
    devices = recv_ref.shape[0]

    def part(source, slot):
        return recv_ref[source, slot].astype(F32)

    def factor(source, prompt):
        slot = 2 * prompts + answers
        high = recv_ref[source, slot, 2 * prompt : 2 * prompt + 1, :].astype(F32)
        low = recv_ref[source, slot, 2 * prompt + 1 : 2 * prompt + 2, :].astype(F32)
        return high + low

    finals = []
    for prompt in range(prompts):
        carried = jnp.zeros(recv_ref.shape[2:], F32)
        for source in range(devices):
            out_ref[source, prompt] = carried.astype(BF16)
            carried = factor(source, prompt) * carried + part(source, prompt)
        finals.append(carried)
    for source in range(devices):
        for answer in range(answers):
            mine = owner[source * answers + answer]
            chosen = finals[0]
            for prompt in range(1, prompts):
                chosen = jnp.where(mine == prompt, finals[prompt], chosen)
            out_ref[source, 2 * prompts + answer] = chosen.astype(BF16)
    for prompt in range(prompts):
        carried = jnp.zeros(recv_ref.shape[2:], F32)
        for source in range(devices):
            for answer in range(answers):
                mine = owner[source * answers + answer]
                carried = carried + jnp.where(mine == prompt, part(source, 2 * prompts + answer), 0.0)
        for source in range(devices - 1, -1, -1):
            out_ref[source, prompts + prompt] = carried.astype(BF16)
            carried = factor(source, prompt) * carried + part(source, prompts + prompt)


def state_of(ref):
    value = ref[:, 0].astype(F32)
    return value.reshape(STATE, value.shape[2]).astype(BF16)


def reverse_sums(value):
    return mm_exact(value, triangle(value.shape[1]), NN)


def prompt_final_kernel(
    start_ref, grad_ref, x_ref, dy_ref, write_ref, read_ref, decay_ref, yin_ref, dxin_ref, dwin_ref, drin_ref, sumin_ref,
    y_ref, dx_ref, dw_ref, dr_ref, dd_ref,
):
    heads = decay_ref.shape[1]
    start, grad = state_of(start_ref), state_of(grad_ref)
    x = x_ref[:, 0].reshape(-1, x_ref.shape[3])
    dy = dy_ref[0].astype(F32)
    write, read = write_ref[0], read_ref[0]
    r = running_columns(decay_ref[0])
    er = spread_heads(jnp.exp(r), heads)
    outside = er * mm(read, start, NN)
    y_ref[0] = (yin_ref[0].astype(F32) + outside).astype(BF16)
    dr_ref[0] = (drin_ref[0] + mm((er * dy).astype(BF16), start, NT)).astype(BF16)
    sums = sumin_ref[0] + head_sums(dy * outside, heads)
    ec = spread_heads(jnp.exp(r[-1:] - r), heads)
    xf = x.astype(F32)
    dw_ref[0] = (dwin_ref[0] + mm((ec * xf).astype(BF16), grad, NT)).astype(BF16)
    moved = ec * mm(write, grad, NN)
    dx_in = dxin_ref[:, 0].reshape(x.shape).astype(F32)
    dx_ref[:, 0] = (dx_in + moved).astype(BF16).reshape(dx_ref.shape[0], dx_ref.shape[2], dx_ref.shape[3])
    pulled = head_sums(xf * moved, heads)
    kept = head_sums(start.astype(F32) * grad.astype(F32), heads)
    closing = jnp.exp(jnp.sum(decay_ref[0], axis=1, keepdims=True)) * jnp.sum(kept, axis=1, keepdims=True)
    size = sums.shape[1]
    dd_ref[0] = reverse_sums(sums) + mm_exact(pulled, triangle(size, False), NN) + closing


def answer_final_kernel(
    limits, start_ref, dy_ref, read_ref, decay_ref, yin_ref, drin_ref, sumin_ref, y_ref, dr_ref, dd_ref
):
    heads = decay_ref.shape[1]
    limit = limits[pl.program_id(0)]
    start = state_of(start_ref)
    dy = masked_rows(dy_ref[0], limit)
    er = spread_heads(jnp.exp(running_columns(decay_ref[0])), heads)
    outside = er * mm(read_ref[0], start, NN)
    y_ref[0] = masked_rows(yin_ref[0].astype(F32) + outside, limit).astype(BF16)
    dr_ref[0] = (drin_ref[0] + mm((er * dy).astype(BF16), start, NT)).astype(BF16)
    dd_ref[0] = reverse_sums(sumin_ref[0] + head_sums(dy * outside, heads))


def per_device(
    prompt_tokens,
    prompt_write,
    prompt_read,
    prompt_decay,
    prompt_cotangent,
    answer_tokens,
    answer_write,
    answer_read,
    answer_decay,
    answer_cotangent,
    group_sizes,
    answer_lengths,
):
    prompts, local_heads, length = prompt_decay.shape
    answers = answer_decay.shape[0]
    groups = prompt_write.shape[2] // STATE
    heads = local_heads // groups
    devices = lax.axis_size("seq")
    split = lax.axis_size("head")
    width, columns = heads * HEAD_DIM, local_heads * HEAD_DIM
    rows, piece = STATE // devices, length // split
    assert length == BLOCK and answer_decay.shape[2] == length

    token = pl.BlockSpec((split, 1, piece, width), lambda s, g, *_: (0, s, 0, g))
    wide = pl.BlockSpec((1, length, width), lambda s, g, *_: (s, 0, g))
    narrow = pl.BlockSpec((1, length, STATE), lambda s, g, *_: (s, 0, g))
    perhead = pl.BlockSpec((1, heads, length), lambda s, g, *_: (s, g, 0))

    def token_at(first):
        return pl.BlockSpec((split, 1, piece, width), lambda s, g, *_: (0, s + first, 0, g))

    def state_at(first):
        return pl.BlockSpec((devices, 1, rows, width), lambda s, g, *_: (0, s + first, 0, g))

    def shape(dims, kind=BF16):
        return jax.ShapeDtypeStruct(dims, kind)

    def call(kernel, count, prefetch, ins, outs, out_shape, name, flops, scratch=(), grid=None):
        return pl.pallas_call(
            kernel,
            grid_spec=pltpu.PrefetchScalarGridSpec(
                num_scalar_prefetch=prefetch,
                grid=grid or (count, groups),
                in_specs=ins,
                out_specs=outs,
                scratch_shapes=list(scratch),
            ),
            out_shape=out_shape,
            compiler_params=PARAMS,
            name=name,
            cost_estimate=pl.CostEstimate(
                flops=flops * count, bytes_accessed=flops * count // 200, transcendentals=0
            ),
        )

    whole = jnp.full((prompts,), length, jnp.int32)
    stacked = jnp.concatenate([prompt_tokens, answer_tokens], axis=0)
    sequences = prompts + answers
    stacked = stacked.reshape(sequences, piece, split, columns).transpose(2, 0, 1, 3)
    x = lax.all_to_all(stacked, "head", split_axis=0, concat_axis=0, tiled=True)

    state_flops = 2 * length * STATE * columns

    def start_grad(count, limits, dy, read, decay, name):
        return call(
            start_grad_kernel, count, 1, [wide, narrow, perhead], state_at(0),
            shape((devices, count, rows, columns)), name, state_flops,
        )(limits, dy, read, decay)

    grad_prompt = start_grad(prompts, whole, prompt_cotangent, prompt_read, prompt_decay, "grad_prompt")
    grad_answer = start_grad(answers, answer_lengths, answer_cotangent, answer_read, answer_decay, "grad_answer")
    end_prompt = call(
        local_end_kernel, prompts, 0, [token_at(0), narrow, perhead], state_at(0),
        shape((devices, prompts, rows, columns)), "end_prompt", state_flops,
    )(x, prompt_write, prompt_decay)

    total = jnp.exp(jnp.sum(prompt_decay, axis=2))
    total_high, total_low = two_term(total)
    pieces = jnp.stack([total_high, total_low], axis=1).reshape(2 * prompts, local_heads)
    pieces = jnp.repeat(pieces, HEAD_DIM, axis=1)
    pieces = jnp.pad(pieces, ((0, rows - 2 * prompts), (0, 0)))
    pieces = jnp.broadcast_to(pieces[None, None], (devices, 1, rows, columns))
    sent = jnp.concatenate([end_prompt, grad_prompt, grad_answer, pieces], axis=1)
    received = lax.all_to_all(sent, "seq", split_axis=0, concat_axis=0, tiled=True)

    def inside(count, limits, first, dy, write, read, decay, kind, name):
        return call(
            inside_kernel, count, 1, [token_at(first), wide, narrow, narrow, perhead],
            [wide, token, narrow, narrow, perhead],
            [
                shape((count, length, columns)),
                shape((split, count, piece, columns)),
                shape((count, length, groups * STATE), kind),
                shape((count, length, groups * STATE), F32),
                shape((count, local_heads, length), F32),
            ],
            name, 8 * length * length * columns,
            (pltpu.VMEM((length, length), F32), pltpu.VMEM((length, width), BF16)),
        )(limits, x, dy, write, read, decay)

    p_y, p_dx, p_dw, p_dr, p_sum = inside(
        prompts, whole, 0, prompt_cotangent, prompt_write, prompt_read, prompt_decay, F32, "inside_prompt"
    )
    a_y, a_dx, a_dw, a_dr, a_sum = inside(
        answers, answer_lengths, prompts, answer_cotangent, answer_write, answer_read, answer_decay, BF16,
        "inside_answer",
    )

    slots = jnp.arange(devices * answers, dtype=jnp.int32)
    bounds = jnp.cumsum(group_sizes)
    owner = jnp.sum((slots[:, None] >= bounds[None, :]).astype(jnp.int32), axis=1)
    states = 2 * prompts + answers
    lanes = 512 if columns % 512 == 0 else columns

    def chain(owner_ref, recv_ref, out_ref):
        chain_kernel(owner_ref, recv_ref, out_ref, prompts=prompts, answers=answers)

    replies = call(
        chain, 1, 1,
        [pl.BlockSpec((devices, states + 1, rows, lanes), lambda c, *_: (0, 0, 0, c))],
        pl.BlockSpec((devices, states, rows, lanes), lambda c, *_: (0, 0, 0, c)),
        shape((devices, states, rows, columns)), "chain", state_flops // 8, (), (columns // lanes,),
    )(owner, received)
    carried = lax.all_to_all(replies, "seq", split_axis=0, concat_axis=0, tiled=True)

    prompt_output, dx, prompt_dw, prompt_dr, prompt_dd = call(
        prompt_final_kernel, prompts, 0,
        [state_at(0), state_at(prompts), token_at(0), wide, narrow, narrow, perhead,
         wide, token, narrow, narrow, perhead],
        [wide, token, narrow, narrow, perhead],
        [
            shape((prompts, length, columns)),
            shape((split, prompts, piece, columns)),
            shape((prompts, length, groups * STATE)),
            shape((prompts, length, groups * STATE)),
            shape((prompts, local_heads, length), F32),
        ],
        "prompt_final", 4 * state_flops,
    )(carried, carried, x, prompt_cotangent, prompt_write, prompt_read, prompt_decay, p_y, p_dx, p_dw, p_dr, p_sum)
    answer_output, answer_dr, answer_dd = call(
        answer_final_kernel, answers, 1,
        [state_at(2 * prompts), wide, narrow, perhead, wide, narrow, perhead],
        [wide, narrow, perhead],
        [
            shape((answers, length, columns)),
            shape((answers, length, groups * STATE)),
            shape((answers, local_heads, length), F32),
        ],
        "answer_final", 2 * state_flops,
    )(answer_lengths, carried, answer_cotangent, answer_read, answer_decay, a_y, a_dr, a_sum)

    def token_back(value):
        back = lax.all_to_all(value, "head", split_axis=0, concat_axis=0, tiled=True)
        return back.transpose(1, 2, 0, 3).reshape(value.shape[1], piece, split * columns)

    return (
        prompt_output,
        token_back(dx),
        prompt_dw,
        prompt_dr,
        prompt_dd,
        answer_output,
        token_back(a_dx),
        a_dw,
        answer_dr,
        answer_dd,
    )


def solution(mesh):
    return jax.shard_map(
        per_device,
        mesh=mesh,
        in_specs=(
            P(None, ("seq", "head"), None),
            P(None, "seq", "head"),
            P(None, "seq", "head"),
            P(None, "head", "seq"),
            P(None, "seq", "head"),
            P("seq", "head", None),
            P("seq", None, "head"),
            P("seq", None, "head"),
            P("seq", "head", None),
            P("seq", None, "head"),
            P(),
            P("seq"),
        ),
        out_specs=(
            P(None, "seq", "head"),
            P(None, ("seq", "head"), None),
            P(None, "seq", "head"),
            P(None, "seq", "head"),
            P(None, "head", "seq"),
            P("seq", None, "head"),
            P("seq", "head", None),
            P("seq", None, "head"),
            P("seq", None, "head"),
            P("seq", "head", None),
        ),
        check_vma=False,
    )
```

time: 873 us -> 276 us (0.32); the launches traced: 861 us -> 275 us
  local copies, waits for them, and re-layouts: 265 us -> 9.87 us
  other arithmetic: 238 us -> 6.03 us
  matrix products: 88.4 us -> 0 us
  Pallas kernels: 0 us -> 74.8 us
  waiting for transfers between devices: 213 us -> 160 us
  blocking collectives: 22.6 us -> 0 us
  between operations: 15.5 us -> 1.41 us
    psum x1 -> x0, waiting for transfers between devices: 147 us -> none  [per_device(): lax.psum(start_local.astype(jnp.bfloat16), 'seq').astype(jnp.float32)]
    all_to_all x4 -> x5, waiting for transfers between devices: 24.6 us -> 160 us  [the longest x1 69.6 us: per_device(): lax.all_to_all(sent, 'seq', split_axis=0, concat_axis=0, tiled=True)]
    select_n x18 -> x0, other arithmetic: 102 us -> none  [the longest x8 47.5 us: absorb_backward(): return jnp.where(source > position, applied, carried)]
    dot_general x24 -> x0, matrix products: 88.4 us -> none  [the longest x22 79.2 us: contract(): jnp.einsum(pattern, first_operand, second_operand, preferred_element_type...]
    pallas_call x0 -> x8, Pallas kernels: none -> 74.8 us  [the longest x2 27.8 us: inside(): call(inside_kernel, count, 1, [token_at(first), wide, narrow, narrow, per...]
    dynamic_slice x32 -> x0, local copies, waits for them, and re-layouts: 72.1 us -> none  [the longest x16 36.4 us: absorb_forward(): every_end[counter]]
    unnamed x149 -> x14, local copies, waits for them, and re-layouts: 69.2 us -> 3.32 us
    unnamed x3 -> x0, other arithmetic: 55.7 us -> none
  transfers between devices with their start and end apart: 7 -> 5, of which waited for: 6 -> 4; matrix products, arithmetic and copies ran while one was open for 39% -> 1% of each run, Pallas kernels for 0% -> 23%
where the time goes in v1:
time: 276 us; the launch traced here: 275 us
  waiting for transfers between devices  160 us (58%)
  Pallas kernels  74.8 us (27%)
  starting transfers between devices  22.8 us (8%)
  local copies, waits for them, and re-layouts  9.87 us (4%)
  other arithmetic  6.03 us (2%)
    all_to_all x1, waiting for transfers between devices, per_device(): lax.all_to_all(sent, 'seq', split_axis=0, concat_axis=0, tiled=True)  69.6 us
    all_to_all x1, waiting for transfers between devices, per_device(): lax.all_to_all(replies, 'seq', split_axis=0, concat_axis=0, tiled=True)  50 us
    pallas_call x2, Pallas kernels, inside(): call(inside_kernel, count, 1, [token_at(first), wide, narrow, narrow, per...  27.8 us
    all_to_all x1, waiting for transfers between devices, per_device(): x = lax.all_to_all(stacked, 'head', split_axis=0, concat_axis=0, tiled=True)  23.3 us
    all_to_all x2, waiting for transfers between devices, token_back(): lax.all_to_all(value, 'head', split_axis=0, concat_axis=0, tiled=True)  17.2 us
    pallas_call x1, Pallas kernels, per_device(): call(prompt_final_kernel, prompts, 0, [state_at(0), state_at(prompts), to...  16 us
    pallas_call x2, Pallas kernels, start_grad(): call(start_grad_kernel, count, 1, [wide, narrow, perhead], state_at(0), s...  12.1 us
    all_to_all x2, starting transfers between devices, token_back(): lax.all_to_all(value, 'head', split_axis=0, concat_axis=0, tiled=True)  8.05 us
  transfers between devices with their start and end apart: 5, of which 4 were waited for; matrix products, arithmetic and copies ran while one was open for 1% of the time, Pallas kernels for 23%

profile of v1, /device:TPU:0, one launch (start us, length us, event | category | flops | bytes accessed | tf_op | source)
XLA Modules:
  0.0 275.2 jit_solution(12930495961673112787)
XLA Ops:
  0.6 2.2 pad_maximum_fusion
  2.8 2.0 copy.35
  4.9 4.4 %all-to-all-start = ((bf16[4,3,64,2048]{3,2,1,0:T(8,128)(2,1)}), bf16[4,3,64,2048]{3,2,1,0:T(8,128)(2,1)S(1)}, u32[]{:S(2)}, u32[]{:S(2)}) async-start(bf16[4,3,64,2048]{3,2,1,0:T(8,128)(2,1)} %bitcast.23), calls=%async_computation | async-start | bytes 6291456 | tf_op jit(solution)/shard_map/all_to_all | solution.py:284
  9.2 0.0 copy-done.5
  9.3 0.1 reduce_sum.19
  9.4 0.1 broadcast_in_dim.4
  9.5 0.1 reshape.90
  10.3 4.4 %grad_answer.1 = bf16[8,1,16,2048]{3,2,1,0:T(8,128)(2,1)} custom-call(s32[1]{0:T(128)S(6)} %copy.36.limits, bf16[1,256,2048]{2,1,0:T(8,128)(2,1)} %dy_ref.11, bf16[1,256,256]{2,1,0:T(8,128)(2,1)} %read_ref.11, f32[1,32,256]{2,1,0:T(8,128)} %decay_ref.13), custom_call_target="tpu_custom_call" | custom-call | flops 134217728 | bytes 671088 | tf_op jit(solution)/shard_map/grad_answer/pallas_call | solution.py:289
  14.7 0.5 broadcast_1_limits.2.limits
  15.2 7.7 %grad_prompt.1 = bf16[8,2,16,2048]{3,2,1,0:T(8,128)(2,1)} custom-call(s32[2]{0:T(128)} %broadcast_1_limits.2.limits, bf16[2,256,2048]{2,1,0:T(8,128)(2,1)} %dy_ref.9, bf16[2,256,256]{2,1,0:T(8,128)(2,1)} %read_ref.9, f32[2,32,256]{2,1,0:T(8,128)} %decay_ref.11), custom_call_target="tpu_custom_call" | custom-call | flops 268435456 | bytes 1342177 | tf_op jit(solution)/shard_map/grad_prompt/pallas_call | solution.py:289
  22.9 23.3 %all-to-all-done.x_ref = bf16[4,3,64,2048]{3,2,1,0:T(8,128)(2,1)S(1)} async-done(((bf16[4,3,64,2048]{3,2,1,0:T(8,128)(2,1)}), bf16[4,3,64,2048]{3,2,1,0:T(8,128)(2,1)S(1)}, u32[]{:S(2)}, u32[]{:S(2)}) %all-to-all-start) | async-done | bytes 3145760 | tf_op jit(solution)/shard_map/all_to_all | solution.py:284
  46.3 1.6 copy-done
  47.9 7.4 %end_prompt.1 = bf16[8,2,16,2048]{3,2,1,0:T(8,128)(2,1)} custom-call(bf16[4,3,64,2048]{3,2,1,0:T(8,128)(2,1)} %copy-done, bf16[2,256,256]{2,1,0:T(8,128)(2,1)} %write_ref.6, f32[2,32,256]{2,1,0:T(8,128)} %decay_ref.11), custom_call_target="tpu_custom_call" | custom-call | flops 268435456 | bytes 1342177 | tf_op jit(solution)/shard_map/end_prompt/pallas_call | solution.py:296
  55.4 2.9 %pad_maximum_fusion.1 = bf16[8,6,16,2048]{3,2,1,0:T(8,128)(2,1)} fusion(bf16[8,1,16,2048]{3,2,1,0:T(8,128)(2,1)S(1)} %broadcast_in_dim.5, bf16[8,1,16,2048]{3,2,1,0:T(8,128)(2,1)S(1)} %copy-done.4, bf16[8,2,16,2048]{3,2,1,0:T(8,128)(2,1)S(1)} %copy-done.3, bf16[8,2,16,2048]{3,2,1,0:T(8,128)(2,1)} %end_prompt.1), kind=kLoop, calls=%fused_computation.2 | loop fusion | flops 4718592 | bytes 6291456 | tf_op jit(solution)/shard_map/concatenate | solution.py:307
  58.3 6.8 %all-to-all-start.1 = ((bf16[8,6,16,2048]{3,2,1,0:T(8,128)(2,1)}), bf16[8,6,16,2048]{3,2,1,0:T(8,128)(2,1)S(1)}, u32[]{:S(2)}, u32[]{:S(2)}) async-start(bf16[8,6,16,2048]{3,2,1,0:T(8,128)(2,1)} %pad_maximum_fusion.1), calls=%async_computation.1 | async-start | bytes 6291456 | tf_op jit(solution)/shard_map/all_to_all | solution.py:308
  65.1 0.2 reduce-window.8
  65.3 0.6 fusion.owner_ref
  65.9 69.6 %all-to-all-done.1.recv_ref = bf16[8,6,16,2048]{3,2,1,0:T(8,128)(2,1)S(1)} async-done(((bf16[8,6,16,2048]{3,2,1,0:T(8,128)(2,1)}), bf16[8,6,16,2048]{3,2,1,0:T(8,128)(2,1)S(1)}, u32[]{:S(2)}, u32[]{:S(2)}) %all-to-all-start.1) | async-done | bytes 3145760 | tf_op jit(solution)/shard_map/all_to_all | solution.py:308
  135.5 1.7 copy-done.2
  137.2 5.3 %chain.1 = bf16[8,5,16,2048]{3,2,1,0:T(8,128)(2,1)} custom-call(s32[8]{0:T(128)} %fusion.owner_ref, bf16[8,6,16,2048]{3,2,1,0:T(8,128)(2,1)} %copy-done.2), custom_call_target="tpu_custom_call" | custom-call | flops 16777216 | bytes 83886 | tf_op jit(solution)/shard_map/chain/pallas_call | solution.py:342
  142.5 3.6 %all-to-all-start.2 = ((bf16[8,5,16,2048]{3,2,1,0:T(8,128)(2,1)}), bf16[8,5,16,2048]{3,2,1,0:T(8,128)(2,1)S(1)}, u32[]{:S(2)}, u32[]{:S(2)}) async-start(bf16[8,5,16,2048]{3,2,1,0:T(8,128)(2,1)} %chain.1), calls=%async_computation.2 | async-start | bytes 5242880 | tf_op jit(solution)/shard_map/all_to_all | solution.py:348
  146.1 9.6 %inside_answer.1 = (bf16[1,256,2048]{2,1,0:T(8,128)(2,1)}, bf16[4,1,64,2048]{3,2,1,0:T(8,128)(2,1)}, bf16[1,256,256]{2,1,0:T(8,128)(2,1)}, f32[1,256,256]{2,1,0:T(8,128)}, f32[1,32,256]{2,1,0:T(8,128)}) custom-call(s32[1]{0:T(128)S(6)} %copy.36.limits, bf16[4,3,64,2048]{3,2,1,0:T(8,128)(2,1)} %copy-done, bf16[1,256,2048]{2,1,0:T(8,128)(2,1)} %dy_ref.11, ...), custom_call_target="tpu_custom_call" | custom-call | flops 1073741824 | bytes 5368709 | tf_op jit(solution)/shard_map/inside_answer/pallas_call | solution.py:311
  155.8 50.0 %all-to-all-done.2.start_ref.grad_ref = bf16[8,5,16,2048]{3,2,1,0:T(8,128)(2,1)S(1)} async-done(((bf16[8,5,16,2048]{3,2,1,0:T(8,128)(2,1)}), bf16[8,5,16,2048]{3,2,1,0:T(8,128)(2,1)S(1)}, u32[]{:S(2)}, u32[]{:S(2)}) %all-to-all-start.2) | async-done | bytes 2621472 | tf_op jit(solution)/shard_map/all_to_all | solution.py:348
  205.8 4.4 %all-to-all-start.4 = ((bf16[4,1,64,2048]{3,2,1,0:T(8,128)(2,1)}), bf16[4,1,64,2048]{3,2,1,0:T(8,128)(2,1)}, u32[]{:S(2)}, u32[]{:S(2)}) async-start(bf16[4,1,64,2048]{3,2,1,0:T(8,128)(2,1)} %get-tuple-element.42), calls=%async_computation.4 | async-start | bytes 2097152 | tf_op jit(solution)/shard_map/all_to_all | solution.py:377
  210.2 18.2 %inside_prompt.1 = (bf16[2,256,2048]{2,1,0:T(8,128)(2,1)}, bf16[4,2,64,2048]{3,2,1,0:T(8,128)(2,1)}, f32[2,256,256]{2,1,0:T(8,128)}, f32[2,256,256]{2,1,0:T(8,128)}, f32[2,32,256]{2,1,0:T(8,128)}) custom-call(s32[2]{0:T(128)} %broadcast_1_limits.2.limits, bf16[4,3,64,2048]{3,2,1,0:T(8,128)(2,1)} %copy-done, bf16[2,256,2048]{2,1,0:T(8,128)(2,1)} %dy_ref.9, ...), custom_call_target="tpu_custom_call" | custom-call | flops 2147483648 | bytes 10737418 | tf_op jit(solution)/shard_map/inside_prompt/pallas_call | solution.py:311
  228.4 16.0 %prompt_final.1 = (bf16[2,256,2048]{2,1,0:T(8,128)(2,1)}, bf16[4,2,64,2048]{3,2,1,0:T(8,128)(2,1)}, bf16[2,256,256]{2,1,0:T(8,128)(2,1)}, bf16[2,256,256]{2,1,0:T(8,128)(2,1)}, f32[2,32,256]{2,1,0:T(8,128)}) custom-call(bf16[8,5,16,2048]{3,2,1,0:T(8,128)(2,1)} %copy-done.1, bf16[8,5,16,2048]{3,2,1,0:T(8,128)(2,1)} %copy-done.1, ...), custom_call_target="tpu_custom_call" | custom-call | flops 1073741824 | bytes 5368709 | tf_op jit(solution)/shard_map/prompt_final/pallas_call | solution.py:350
  244.4 0.0 all-to-all-done.4
  244.4 3.6 %all-to-all-start.3 = ((bf16[4,2,64,2048]{3,2,1,0:T(8,128)(2,1)}), bf16[4,2,64,2048]{3,2,1,0:T(8,128)(2,1)S(1)}, u32[]{:S(2)}, u32[]{:S(2)}) async-start(bf16[4,2,64,2048]{3,2,1,0:T(8,128)(2,1)} %get-tuple-element.34), calls=%async_computation.3 | async-start | bytes 4194304 | tf_op jit(solution)/shard_map/all_to_all | solution.py:377
  248.1 2.3 copy.33
  250.4 6.1 %answer_final.1 = (bf16[1,256,2048]{2,1,0:T(8,128)(2,1)}, bf16[1,256,256]{2,1,0:T(8,128)(2,1)}, f32[1,32,256]{2,1,0:T(8,128)}) custom-call(s32[1]{0:T(128)S(6)} %copy.36.limits, bf16[8,5,16,2048]{3,2,1,0:T(8,128)(2,1)} %copy-done.1, bf16[1,256,2048]{2,1,0:T(8,128)(2,1)} %dy_ref.11, bf16[1,256,256]{2,1,0:T(8,128)(2,1)} %read_ref.11, ...), custom_call_target="tpu_custom_call" | custom-call | flops 268435456 | bytes 1342177 | tf_op jit(solution)/shard_map/answer_final/pallas_call | solution.py:364
  256.5 17.2 %all-to-all-done.3 = bf16[4,2,64,2048]{3,2,1,0:T(8,128)(2,1)S(1)} async-done(((bf16[4,2,64,2048]{3,2,1,0:T(8,128)(2,1)}), bf16[4,2,64,2048]{3,2,1,0:T(8,128)(2,1)S(1)}, u32[]{:S(2)}, u32[]{:S(2)}) %all-to-all-start.3) | async-done | bytes 2097184 | tf_op jit(solution)/shard_map/all_to_all | solution.py:377
  273.7 1.5 copy.32
  (17 shorter events, 0.1 us)
Async XLA Ops:
  4.9 4.4 %copy-start.5 = (f32[2,32,256]{2,1,0:T(8,128)S(1)}, f32[2,32,256]{2,1,0:T(8,128)}, u32[]{:S(2)}) copy-start(f32[2,32,256]{2,1,0:T(8,128)} %decay_ref.11) | copy-start | bytes 196612
  4.9 41.4 %all-to-all-start = ((bf16[4,3,64,2048]{3,2,1,0:T(8,128)(2,1)}), bf16[4,3,64,2048]{3,2,1,0:T(8,128)(2,1)S(1)}, u32[]{:S(2)}, u32[]{:S(2)}) async-start(bf16[4,3,64,2048]{3,2,1,0:T(8,128)(2,1)} %bitcast.23), calls=%async_computation | async-start | bytes 6291456 | tf_op jit(solution)/shard_map/all_to_all | solution.py:284
  46.3 1.6 copy-start
  47.9 7.5 %copy-start.3 = (bf16[8,2,16,2048]{3,2,1,0:T(8,128)(2,1)S(1)}, bf16[8,2,16,2048]{3,2,1,0:T(8,128)(2,1)}, u32[]{:S(2)}) copy-start(bf16[8,2,16,2048]{3,2,1,0:T(8,128)(2,1)} %grad_prompt.1) | copy-start | bytes 3145732
  47.9 7.5 %copy-start.4 = (bf16[8,1,16,2048]{3,2,1,0:T(8,128)(2,1)S(1)}, bf16[8,1,16,2048]{3,2,1,0:T(8,128)(2,1)}, u32[]{:S(2)}) copy-start(bf16[8,1,16,2048]{3,2,1,0:T(8,128)(2,1)} %grad_answer.1) | copy-start | bytes 1572868
  58.3 6.8 %copy-start.6 = (s32[2]{0:T(128)S(1)}, s32[2]{0:T(128)}, u32[]{:S(2)}) copy-start(s32[2]{0:T(128)} %param.22) | copy-start | bytes 28
  58.3 77.2 %all-to-all-start.1 = ((bf16[8,6,16,2048]{3,2,1,0:T(8,128)(2,1)}), bf16[8,6,16,2048]{3,2,1,0:T(8,128)(2,1)S(1)}, u32[]{:S(2)}, u32[]{:S(2)}) async-start(bf16[8,6,16,2048]{3,2,1,0:T(8,128)(2,1)} %pad_maximum_fusion.1), calls=%async_computation.1 | async-start | bytes 6291456 | tf_op jit(solution)/shard_map/all_to_all | solution.py:308
  135.5 1.7 copy-start.2
  142.5 63.3 %all-to-all-start.2 = ((bf16[8,5,16,2048]{3,2,1,0:T(8,128)(2,1)}), bf16[8,5,16,2048]{3,2,1,0:T(8,128)(2,1)S(1)}, u32[]{:S(2)}, u32[]{:S(2)}) async-start(bf16[8,5,16,2048]{3,2,1,0:T(8,128)(2,1)} %chain.1), calls=%async_computation.2 | async-start | bytes 5242880 | tf_op jit(solution)/shard_map/all_to_all | solution.py:348
  205.8 22.6 %copy-start.1 = (bf16[8,5,16,2048]{3,2,1,0:T(8,128)(2,1)}, bf16[8,5,16,2048]{3,2,1,0:T(8,128)(2,1)S(1)}, u32[]{:S(2)}) copy-start(bf16[8,5,16,2048]{3,2,1,0:T(8,128)(2,1)S(1)} %all-to-all-done.2.start_ref.grad_ref) | copy-start | bytes 7864324
  205.8 38.6 %all-to-all-start.4 = ((bf16[4,1,64,2048]{3,2,1,0:T(8,128)(2,1)}), bf16[4,1,64,2048]{3,2,1,0:T(8,128)(2,1)}, u32[]{:S(2)}, u32[]{:S(2)}) async-start(bf16[4,1,64,2048]{3,2,1,0:T(8,128)(2,1)} %get-tuple-element.42), calls=%async_computation.4 | async-start | bytes 2097152 | tf_op jit(solution)/shard_map/all_to_all | solution.py:377
  244.4 29.3 %all-to-all-start.3 = ((bf16[4,2,64,2048]{3,2,1,0:T(8,128)(2,1)}), bf16[4,2,64,2048]{3,2,1,0:T(8,128)(2,1)S(1)}, u32[]{:S(2)}, u32[]{:S(2)}) async-start(bf16[4,2,64,2048]{3,2,1,0:T(8,128)(2,1)} %get-tuple-element.34), calls=%async_computation.3 | async-start | bytes 4194304 | tf_op jit(solution)/shard_map/all_to_all | solution.py:377
